TPU v7x, 32 devices: a whole 2x2x4 slice. The times are simulated.
32 devices in a mesh: grp: 2 (over y), ctx: 16 (over z, x, core).
Axes of the slice: x: 2, y: 2, z: 4, core: 2. Of those that a mesh axis runs over, the one named last changes fastest.
Arguments:
- query_rows: bfloat16 [4096, 4096], P(('grp', 'ctx')), parts along dimension 0, may hold values from -6 to 6
- key_rows: bfloat16 [4096, 4096], P(('grp', 'ctx')), parts along dimension 0, may hold values from -6 to 6
- value_rows: bfloat16 [4096, 4096], P(('grp', 'ctx')), parts along dimension 0, may hold values from -6 to 6
- grad_out: bfloat16 [4096, 4096], P(('grp', 'ctx')), parts along dimension 0, may hold values from -6 to 6
- conv_filter: bfloat16 [256, 128], replicated, may hold values from -0.44194174 to 0.44194174
Outputs:
- grad_query: bfloat16 [4096, 4096], P(('grp', 'ctx')), parts along dimension 0
- grad_key: bfloat16 [4096, 4096], P(('grp', 'ctx')), parts along dimension 0
- grad_value: bfloat16 [4096, 4096], P(('grp', 'ctx')), parts along dimension 0
- grad_filter: float32 [512, 128], P(('grp', 'ctx')), parts along dimension 0
There are 2 independent parts, one for each index of `grp`. A program takes and returns all parts, laid end to end along the dimension named above; an argument that names none is the same for every part. Nothing has to cross between parts.
All inputs are finite; a program needn't handle non-finite values.
Results may differ from a plain program's by a relative error of at most 0.005.
Values may be sent and summed in bfloat16 or wider, within the bound.
No kernel may reach another device: no remote copies, remote signals or barrier semaphores. Data moves between devices by JAX's collectives and lax.ppermute only.
A program may use at most 64 MiB of HBM per device.

v0:
```python
import math
import jax
import jax.numpy as jnp
from jax import lax
from jax.sharding import PartitionSpec as P

GSIZE = 16
TAPS = 128


def toeplitz(filter_rows, offsets):
    taps_index = lax.broadcasted_iota(jnp.int32, offsets.shape + (TAPS,), 2)
    selector = (offsets[:, :, None] == taps_index).astype(filter_rows.dtype)
    picked = jnp.einsum("gj,tsj->gts", filter_rows, selector, preferred_element_type=jnp.float32)
    return picked.astype(filter_rows.dtype)


def block_terms(prod_now, prod_before, grad_now, grad_after, filter_rows):
    block_total, block_rows, channels = prod_now.shape
    rim_rows = prod_before.shape[1]
    groups_here = channels // GSIZE
    row_index = lax.broadcasted_iota(jnp.int32, (block_rows, block_rows + rim_rows), 0)
    col_index = lax.broadcasted_iota(jnp.int32, (block_rows, block_rows + rim_rows), 1)
    causal = toeplitz(filter_rows, rim_rows + row_index - col_index)
    future = toeplitz(filter_rows, col_index - row_index)
    extended = jnp.concatenate([prod_before, prod_now], axis=1).reshape(
        block_total, block_rows + rim_rows, groups_here, GSIZE
    )
    grads_ahead = jnp.concatenate([grad_now, grad_after], axis=1).reshape(
        block_total, block_rows + rim_rows, groups_here, GSIZE
    )
    mixed_sum = jnp.einsum("gts,bsgc->btgc", causal, extended, preferred_element_type=jnp.float32)
    back_sum = jnp.einsum("gts,bsgc->btgc", future, grads_ahead, preferred_element_type=jnp.float32)
    grads_here = grad_now.reshape(block_total, block_rows, groups_here, GSIZE)
    pair_sums = jnp.einsum(
        "btgc,bsgc->gts", grads_here, extended, preferred_element_type=jnp.float32
    )
    flattened = pair_sums.reshape(groups_here, block_rows * (block_rows + rim_rows))
    flattened = jnp.pad(flattened, ((0, 0), (0, block_rows)))
    skewed = flattened.reshape(groups_here, block_rows, block_rows + rim_rows + 1)
    picked = skewed[:, :, rim_rows - TAPS + 1 : rim_rows + 1]
    filter_part = jnp.flip(jnp.sum(picked, axis=1), axis=1)
    shape_out = (block_total, block_rows, channels)
    return (mixed_sum.reshape(shape_out), back_sum.reshape(shape_out), filter_part)


def window_terms(prod_now, prod_before, grad_now, grad_after, filter_rows, sub_rows):
    block_total, block_rows, channels = prod_now.shape
    sub_count = block_rows // sub_rows
    prod_full = jnp.concatenate([prod_before, prod_now], axis=1)
    prod_full = prod_full.reshape(block_total, (block_rows + TAPS) // sub_rows, sub_rows, channels)
    grad_full = jnp.concatenate([grad_now, grad_after], axis=1)
    grad_full = grad_full.reshape(block_total, (block_rows + TAPS) // sub_rows, sub_rows, channels)
    before_win = prod_full[:, 0:sub_count]
    after_win = grad_full[:, 1 : 1 + sub_count]
    flat_count = block_total * sub_count
    mixed_sum, back_sum, filter_part = block_terms(
        prod_now,
        before_win.reshape(flat_count, TAPS, channels),
        grad_now,
        after_win.reshape(flat_count, TAPS, channels),
        filter_rows,
    )
    return (mixed_sum, back_sum, filter_part)


def run_blocks(prod_now, prod_before, grad_now, grad_after, filter_rows, sub_rows):
    block_total, block_rows, channels = prod_now.shape
    block_width = min(512, channels)
    block_count = channels // block_width

    def to_blocks(array):
        return jnp.moveaxis(
            array.reshape(array.shape[0], array.shape[1], block_count, block_width), 2, 0
        )

    def from_blocks(array):
        return jnp.moveaxis(array, 0, 2).reshape(block_total, block_rows, channels)

    def one_block(block_items):
        return window_terms(
            block_items[0], block_items[1], block_items[2], block_items[3], block_items[4], sub_rows
        )

    block_items = (
        to_blocks(prod_now),
        to_blocks(prod_before),
        to_blocks(grad_now),
        to_blocks(grad_after),
        filter_rows.reshape(block_count, block_width // GSIZE, TAPS),
    )
    mixed_sum, back_sum, filter_part = lax.map(one_block, block_items)
    return (
        from_blocks(mixed_sum),
        from_blocks(back_sum),
        filter_part.reshape(channels // GSIZE, TAPS),
    )


def shards(query_rows, key_rows, value_rows, grad_out, conv_filter):
    product = (key_rows.astype(jnp.float32) * value_rows.astype(jnp.float32)).astype(jnp.bfloat16)
    gated_grad = (grad_out.astype(jnp.float32) * query_rows.astype(jnp.float32)).astype(
        jnp.bfloat16
    )
    local_rows = product.shape[0]
    moved_prod, moved_grad = (
        lax.all_to_all(product, "ctx", split_axis=1, concat_axis=0, tiled=True),
        lax.all_to_all(gated_grad, "ctx", split_axis=1, concat_axis=0, tiled=True),
    )
    total_rows, channels = moved_prod.shape
    block_total = total_rows // TAPS
    blocks_prod = moved_prod.reshape(block_total, TAPS, channels)
    blocks_grad = moved_grad.reshape(block_total, TAPS, channels)
    zero_block = jnp.zeros((1, TAPS, channels), jnp.bfloat16)
    rows_before = jnp.concatenate([zero_block, blocks_prod[:-1]], axis=0)
    rows_after = jnp.concatenate([blocks_grad[1:], zero_block], axis=0)
    groups_here = channels // GSIZE
    own_filter = lax.dynamic_slice_in_dim(
        conv_filter, lax.axis_index("ctx") * groups_here, groups_here, 0
    )
    mixed_sum, back_sum, filter_part = run_blocks(
        blocks_prod, rows_before, blocks_grad, rows_after, own_filter, TAPS
    )
    mixed_sum = mixed_sum.reshape(total_rows, channels)
    back_sum = back_sum.reshape(total_rows, channels)
    mixed_home, back_home = (
        lax.all_to_all(mixed_sum, "ctx", split_axis=0, concat_axis=1, tiled=True),
        lax.all_to_all(back_sum, "ctx", split_axis=0, concat_axis=1, tiled=True),
    )
    grad_scale = 1.0 / math.sqrt(local_rows * lax.axis_size("ctx") * GSIZE)
    grad_query = (grad_out.astype(jnp.float32) * mixed_home).astype(jnp.bfloat16)
    grad_key = (back_home * value_rows.astype(jnp.float32)).astype(jnp.bfloat16)
    grad_value = (back_home * key_rows.astype(jnp.float32)).astype(jnp.bfloat16)
    return (grad_query, grad_key, grad_value, filter_part * grad_scale)


def solution(mesh):
    return jax.shard_map(
        shards,
        mesh=mesh,
        in_specs=(
            P(("grp", "ctx"), None),
            P(("grp", "ctx"), None),
            P(("grp", "ctx"), None),
            P(("grp", "ctx"), None),
            P(),
        ),
        out_specs=(
            P(("grp", "ctx"), None),
            P(("grp", "ctx"), None),
            P(("grp", "ctx"), None),
            P(("grp", "ctx"), None),
        ),
        check_vma=False,
    )
```

profile of v0, /device:TPU:15, one launch (start us, length us, event | category | flops | bytes accessed | tf_op | source)
XLA Modules:
  0.0 199.6 jit_solution(10627907065178947283)
XLA Ops:
  0.6 1.8 fusion.7
  2.5 1.3 copy.47
  3.8 6.5 %all-to-all-start.2 = ((bf16[128,16,256]{0,2,1:T(8,128)(2,1)}), bf16[128,16,256]{0,2,1:T(8,128)(2,1)S(1)}, u32[]{:S(2)}, u32[]{:S(2)}) async-start(bf16[128,16,256]{0,2,1:T(8,128)(2,1)} %bitcast.11), calls=%async_computation.2 | async-start | bytes 2097152 | tf_op jit(solution)/shard_map/all_to_all | solution.py:108
  10.3 8.2 %fusion.26 = bf16[16,128,256,1]{2,0,1,3:T(8,128)(2,1)} fusion(s32[128,256]{1,0:T(8,128)S(1)} %iota_subtract_fusion, bf16[256,128]{1,0:T(8,128)(2,1)S(1)} %copy-done, s32[]{:T(128)S(6)} %select_n.3), kind=kOutput, calls=%fused_computation.33 | convolution fusion | flops 138936320 | bytes 1183748 | tf_op jit(solution)/shard_map/while/body/eval_jaxpr/gj,tsj->gts/dot_general | solution.py:14
  18.5 16.7 %all-to-all-done.2 = bf16[128,16,256]{0,2,1:T(8,128)(2,1)S(1)} async-done(((bf16[128,16,256]{0,2,1:T(8,128)(2,1)}), bf16[128,16,256]{0,2,1:T(8,128)(2,1)S(1)}, u32[]{:S(2)}, u32[]{:S(2)}) %all-to-all-start.2) | async-done | bytes 1048608 | tf_op jit(solution)/shard_map/all_to_all | solution.py:108
  35.5 2.1 %reshape.111 = bf16[16,2,128,256]{2,1,3,0:T(2,128)(2,1)} reshape(bf16[16,256,256]{1,2,0:T(8,128)(2,1)S(1)} %fusion.11) | data formatting | bytes 4194304 | tf_op jit(solution)/shard_map/while/body/eval_jaxpr/reshape | solution.py:53
  37.6 4.0 %slice.28 = bf16[16,1,128,256]{2,1,3,0:T(2,128)(2,1)S(1)} slice(bf16[16,2,128,256]{2,1,3,0:T(2,128)(2,1)} %reshape.111), slice={[0:16], [1:2], [0:128], [0:256]} | slice | bytes 2097152 | tf_op jit(solution)/shard_map/while/body/eval_jaxpr/slice | solution.py:55
  43.5 1.6 copy.52
  45.1 4.8 %all-to-all-start.3 = ((f32[16,128,256]{1,2,0:T(8,128)}), f32[16,128,256]{1,2,0:T(8,128)S(1)}, u32[]{:S(2)}, u32[]{:S(2)}) async-start(f32[16,128,256]{1,2,0:T(8,128)} %bitcast.49), calls=%async_computation.3 | async-start | bytes 4194304 | tf_op jit(solution)/shard_map/all_to_all | solution.py:128
  49.9 2.3 %copy.38 = bf16[128,4096]{0,1:T(8,128)(2,1)} copy(bf16[128,4096]{1,0:T(8,128)(2,1)} %param.6) | data formatting | bytes 2097152 | tf_op args[1]
  52.2 2.3 %copy.39 = bf16[128,4096]{0,1:T(8,128)(2,1)} copy(bf16[128,4096]{1,0:T(8,128)(2,1)} %param.7) | data formatting | bytes 2097152 | tf_op args[2]
  54.5 42.9 %all-to-all-done.3 = f32[16,128,256]{1,2,0:T(8,128)S(1)} async-done(((f32[16,128,256]{1,2,0:T(8,128)}), f32[16,128,256]{1,2,0:T(8,128)S(1)}, u32[]{:S(2)}, u32[]{:S(2)}) %all-to-all-start.3) | async-done | bytes 2097184 | tf_op jit(solution)/shard_map/all_to_all | solution.py:128
  97.4 3.6 %fusion.8 = (bf16[128,4096]{0,1:T(8,128)(2,1)}, bf16[128,4096]{0,1:T(8,128)(2,1)}, bf16[128,4096]{0,1:T(8,128)(2,1)}) fusion(bf16[128,4096]{0,1:T(8,128)(2,1)} %copy.38, f32[16,128,256]{1,2,0:T(8,128)S(1)} %all-to-all-done.3, bf16[128,4096]{0,1:T(8,128)(2,1)} %copy.39), kind=kLoop, calls=%fused_computation.17 | loop fusion | flops 4194304 | bytes 7340032 | tf_op jit(solution)/shard_map/convert_element_type | solution.py:133
  100.9 4.8 %all-to-all-start = ((bf16[128,16,256]{0,2,1:T(8,128)(2,1)}), bf16[128,16,256]{0,2,1:T(8,128)(2,1)S(1)}, u32[]{:S(2)}, u32[]{:S(2)}) async-start(bf16[128,16,256]{0,2,1:T(8,128)(2,1)} %bitcast.55), calls=%async_computation | async-start | bytes 2097152 | tf_op jit(solution)/shard_map/all_to_all | solution.py:107
  105.8 8.2 %fusion.25 = bf16[16,128,256,1]{2,0,1,3:T(8,128)(2,1)} fusion(s32[128,256]{1,0:T(8,128)S(1)} %iota_subtract_fusion.1, bf16[256,128]{1,0:T(8,128)(2,1)S(1)} %copy-done, s32[]{:T(128)S(6)} %select_n.3), kind=kOutput, calls=%fused_computation.32 | convolution fusion | flops 138936320 | bytes 1183748 | tf_op jit(solution)/shard_map/while/body/eval_jaxpr/gj,tsj->gts/dot_general | solution.py:14
  114.0 16.6 %all-to-all-done = bf16[128,16,256]{0,2,1:T(8,128)(2,1)S(1)} async-done(((bf16[128,16,256]{0,2,1:T(8,128)(2,1)}), bf16[128,16,256]{0,2,1:T(8,128)(2,1)S(1)}, u32[]{:S(2)}, u32[]{:S(2)}) %all-to-all-start) | async-done | bytes 1048608 | tf_op jit(solution)/shard_map/all_to_all | solution.py:107
  130.7 1.6 fusion.12
  132.2 3.9 %copy.40 = bf16[16,256,256]{2,1,0:T(8,128)(2,1)} copy(bf16[16,256,256]{1,2,0:T(8,128)(2,1)} %fusion.12) | data formatting | bytes 4194304 | tf_op jit(solution)/shard_map/while/body/eval_jaxpr/concatenate | solution.py:50
  136.2 2.3 %slice.26 = bf16[16,1,128,256]{3,2,1,0:T(8,128)(2,1)} slice(bf16[16,2,128,256]{3,2,1,0:T(8,128)(2,1)} %bitcast.52), slice={[0:16], [0:1], [0:128], [0:256]} | slice | bytes 2097152 | tf_op jit(solution)/shard_map/while/body/eval_jaxpr/slice | solution.py:54
  138.5 1.6 copy.41
  140.1 2.3 %fusion.17 = f32[16,128,16,16]{1,3,0,2:T(8,128)S(1)} fusion(bf16[16,128,256,1]{2,0,1,3:T(8,128)(2,1)} %fusion.25, bf16[16,128,16,16]{1,3,2,0:T(8,128)(2,1)S(1)} %bitcast.46, bf16[16,128,16,16]{1,3,2,0:T(8,128)(2,1)S(1)} %bitcast.53), kind=kOutput, calls=%fused_computation.28 | convolution fusion | flops 272629760 | bytes 5242880 | tf_op jit(solution)/shard_map/while/body/eval_jaxpr/gts,bsgc->btgc/dot_general | solution.py:32
  142.4 1.6 copy.45
  144.0 4.8 %all-to-all-start.1 = ((f32[16,128,256]{1,2,0:T(8,128)}), f32[16,128,256]{1,2,0:T(8,128)}, u32[]{:S(2)}, u32[]{:S(2)}) async-start(f32[16,128,256]{1,2,0:T(8,128)} %bitcast.48), calls=%async_computation.1 | async-start | bytes 4194304 | tf_op jit(solution)/shard_map/all_to_all | solution.py:127
  148.8 2.4 %copy.55 = bf16[128,4096]{1,0:T(8,128)(2,1)} copy(bf16[128,4096]{0,1:T(8,128)(2,1)} %get-tuple-element.26) | data formatting | bytes 2097152
  151.2 1.3 copy.54
  152.5 1.7 fusion.35
  154.2 1.2 copy.65
  155.6 3.6 %reshape.113 = f32[16,128,257]{2,1,0:T(8,128)} reshape(f32[16,32896]{1,0:T(8,128)S(1)} %pad.7) | data formatting | bytes 4210688 | tf_op jit(solution)/shard_map/while/body/eval_jaxpr/reshape | solution.py:40
  159.3 1.9 slice_reduce_fusion
  161.9 34.5 %all-to-all-done.1 = f32[16,128,256]{1,2,0:T(8,128)} async-done(((f32[16,128,256]{1,2,0:T(8,128)}), f32[16,128,256]{1,2,0:T(8,128)}, u32[]{:S(2)}, u32[]{:S(2)}) %all-to-all-start.1) | async-done | bytes 2097184 | tf_op jit(solution)/shard_map/all_to_all | solution.py:127
  196.4 2.0 %copy.46 = f32[128,4096]{1,0:T(8,128)S(1)} copy(f32[128,4096]{0,1:T(8,128)} %bitcast.10) | data formatting | bytes 4194304 | tf_op jit(solution)/shard_map/all_to_all | solution.py:127
  198.4 1.2 fusion.6
  (21 shorter events, 3.3 us)
Async XLA Ops:
  0.6 9.7 %copy-start = (bf16[256,128]{1,0:T(8,128)(2,1)S(1)}, bf16[256,128]{1,0:T(8,128)(2,1)}, u32[]{:S(2)}) copy-start(bf16[256,128]{1,0:T(8,128)(2,1)} %param.9) | copy-start | bytes 196612
  3.8 31.4 %all-to-all-start.2 = ((bf16[128,16,256]{0,2,1:T(8,128)(2,1)}), bf16[128,16,256]{0,2,1:T(8,128)(2,1)S(1)}, u32[]{:S(2)}, u32[]{:S(2)}) async-start(bf16[128,16,256]{0,2,1:T(8,128)(2,1)} %bitcast.11), calls=%async_computation.2 | async-start | bytes 2097152 | tf_op jit(solution)/shard_map/all_to_all | solution.py:108
  41.6 1.2 copy-start.4
  45.1 52.2 %all-to-all-start.3 = ((f32[16,128,256]{1,2,0:T(8,128)}), f32[16,128,256]{1,2,0:T(8,128)S(1)}, u32[]{:S(2)}, u32[]{:S(2)}) async-start(f32[16,128,256]{1,2,0:T(8,128)} %bitcast.49), calls=%async_computation.3 | async-start | bytes 4194304 | tf_op jit(solution)/shard_map/all_to_all | solution.py:128
  100.9 29.6 %all-to-all-start = ((bf16[128,16,256]{0,2,1:T(8,128)(2,1)}), bf16[128,16,256]{0,2,1:T(8,128)(2,1)S(1)}, u32[]{:S(2)}, u32[]{:S(2)}) async-start(bf16[128,16,256]{0,2,1:T(8,128)(2,1)} %bitcast.55), calls=%async_computation | async-start | bytes 2097152 | tf_op jit(solution)/shard_map/all_to_all | solution.py:107
  140.1 2.3 %copy-start.2 = (bf16[16,1,128,256]{2,3,0,1:T(8,128)(2,1)}, bf16[16,1,128,256]{2,3,0,1:T(8,128)(2,1)S(1)}, u32[]{:S(2)}) copy-start(bf16[16,1,128,256]{2,3,0,1:T(8,128)(2,1)S(1)} %copy.41) | copy-start | bytes 3145732
  144.0 52.4 %all-to-all-start.1 = ((f32[16,128,256]{1,2,0:T(8,128)}), f32[16,128,256]{1,2,0:T(8,128)}, u32[]{:S(2)}, u32[]{:S(2)}) async-start(f32[16,128,256]{1,2,0:T(8,128)} %bitcast.48), calls=%async_computation.1 | async-start | bytes 4194304 | tf_op jit(solution)/shard_map/all_to_all | solution.py:127
  148.8 2.4 %copy-start.1 = (bf16[128,4096]{0,1:T(8,128)(2,1)S(1)}, bf16[128,4096]{0,1:T(8,128)(2,1)}, u32[]{:S(2)}) copy-start(bf16[128,4096]{0,1:T(8,128)(2,1)} %get-tuple-element.36) | copy-start | bytes 3145732
  196.4 2.0 %copy-start.3 = (bf16[128,4096]{1,0:T(8,128)(2,1)S(1)}, bf16[128,4096]{1,0:T(8,128)(2,1)}, u32[]{:S(2)}) copy-start(bf16[128,4096]{1,0:T(8,128)(2,1)} %param.8) | copy-start | bytes 3145732
where the time goes:
time: 200 us
  waiting for transfers between devices  111 us (56%)
  local copies, waits for them, and re-layouts  35 us (18%)
  matrix products  21.1 us (11%)
  starting transfers between devices  21 us (10%)
  other arithmetic  11.1 us (6%)
    all_to_all x1, waiting for transfers between devices, shards(): lax.all_to_all(back_sum, 'ctx', split_axis=0, concat_axis=1, tiled=True)  42.9 us
    all_to_all x1, waiting for transfers between devices, shards(): lax.all_to_all(mixed_sum, 'ctx', split_axis=0, concat_axis=1, tiled=True)  34.5 us
    all_to_all x1, waiting for transfers between devices, shards(): lax.all_to_all(gated_grad, 'ctx', split_axis=1, concat_axis=0, tiled=True)  16.7 us
    all_to_all x1, waiting for transfers between devices, shards(): lax.all_to_all(product, 'ctx', split_axis=1, concat_axis=0, tiled=True)  16.6 us
    dot_general x2, matrix products, toeplitz(): jnp.einsum('gj,tsj->gts', filter_rows, selector, preferred_element_type=j...  16.3 us
    unnamed x16, local copies, waits for them, and re-layouts  10.6 us
    all_to_all x1, starting transfers between devices, shards(): lax.all_to_all(gated_grad, 'ctx', split_axis=1, concat_axis=0, tiled=True)  6.52 us
    all_to_all x1, starting transfers between devices, shards(): lax.all_to_all(back_sum, 'ctx', split_axis=0, concat_axis=1, tiled=True)  4.83 us
  transfers between devices with their start and end apart: 4, of which 4 were waited for; matrix products, arithmetic and copies ran while one was open for 17% of the time, Pallas kernels for 0%

commit v1 on v0

--- a/solution.py
+++ b/solution.py
@@ -6,6 +6,22 @@
 
 GSIZE = 16
 TAPS = 128
+
+
+def pairwise_exchange(array, axis, split, join):
+    ways, here = (lax.axis_size(axis), lax.axis_index(axis))
+    width = array.shape[split] // ways
+    dims = list(array.shape)
+    dims[split] = width
+    height = dims[join]
+    dims[join] = height * ways
+    full = jnp.zeros(dims, array.dtype)
+    for mask in range(ways):
+        part = lax.dynamic_slice_in_dim(array, (here ^ mask) * width, width, axis=split)
+        if mask:
+            part = lax.ppermute(part, axis, [(d, d ^ mask) for d in range(ways)])
+        full = lax.dynamic_update_slice_in_dim(full, part, (here ^ mask) * height, axis=join)
+    return full
 
 
 def toeplitz(filter_rows, offsets):
@@ -125,7 +141,7 @@
     back_sum = back_sum.reshape(total_rows, channels)
     mixed_home, back_home = (
         lax.all_to_all(mixed_sum, "ctx", split_axis=0, concat_axis=1, tiled=True),
-        lax.all_to_all(back_sum, "ctx", split_axis=0, concat_axis=1, tiled=True),
+        pairwise_exchange(back_sum, "ctx", 0, 1),
     )
     grad_scale = 1.0 / math.sqrt(local_rows * lax.axis_size("ctx") * GSIZE)
     grad_query = (grad_out.astype(jnp.float32) * mixed_home).astype(jnp.bfloat16)

time: 200 us -> 209 us (1.045)
  starting transfers between devices: 21 us -> 34 us
  waiting for transfers between devices: 111 us -> 104 us
  local copies, waits for them, and re-layouts: 35 us -> 38.3 us
    all_to_all x1 -> x0, waiting for transfers between devices: 42.9 us -> none  [shards(): lax.all_to_all(back_sum, 'ctx', split_axis=0, concat_axis=1, tiled=True)]
    ppermute x0 -> x15, waiting for transfers between devices: none -> 36.5 us  [pairwise_exchange(): part = lax.ppermute(part, axis, [(d, d ^ mask) for d in range(ways)])]
    ppermute x0 -> x15, starting transfers between devices: none -> 17.6 us  [pairwise_exchange(): part = lax.ppermute(part, axis, [(d, d ^ mask) for d in range(ways)])]
    all_to_all x1 -> x0, starting transfers between devices: 4.83 us -> none  [shards(): lax.all_to_all(back_sum, 'ctx', split_axis=0, concat_axis=1, tiled=True)]
    unnamed x16 -> x21, local copies, waits for them, and re-layouts: 10.6 us -> 11.5 us
  transfers between devices with their start and end apart: 4 -> 18, of which waited for: 4 -> 11; matrix products, arithmetic and copies ran while one was open for 17% -> 17% of each run, Pallas kernels for 0% -> 0%
where the time goes in v1:
time: 209 us; the launch traced here: 208 us
  waiting for transfers between devices  104 us (50%)
  local copies, waits for them, and re-layouts  38.3 us (18%)
  starting transfers between devices  34 us (16%)
  matrix products  21.2 us (10%)
  other arithmetic  9.58 us (5%)
    ppermute x15, waiting for transfers between devices, pairwise_exchange(): part = lax.ppermute(part, axis, [(d, d ^ mask) for d in range(ways)])  36.5 us
    all_to_all x1, waiting for transfers between devices, shards(): lax.all_to_all(mixed_sum, 'ctx', split_axis=0, concat_axis=1, tiled=True)  34.5 us
    ppermute x15, starting transfers between devices, pairwise_exchange(): part = lax.ppermute(part, axis, [(d, d ^ mask) for d in range(ways)])  17.6 us
    all_to_all x1, waiting for transfers between devices, shards(): lax.all_to_all(gated_grad, 'ctx', split_axis=1, concat_axis=0, tiled=True)  16.7 us
    all_to_all x1, waiting for transfers between devices, shards(): lax.all_to_all(product, 'ctx', split_axis=1, concat_axis=0, tiled=True)  16.6 us
    dot_general x2, matrix products, toeplitz(): jnp.einsum('gj,tsj->gts', filter_rows, selector, preferred_element_type=j...  16.3 us
    unnamed x21, local copies, waits for them, and re-layouts  11.5 us
    all_to_all x1, starting transfers between devices, shards(): lax.all_to_all(gated_grad, 'ctx', split_axis=1, concat_axis=0, tiled=True)  6.52 us
  transfers between devices with their start and end apart: 18, of which 11 were waited for; matrix products, arithmetic and copies ran while one was open for 17% of the time, Pallas kernels for 0%

profile of v1, /device:TPU:15, one launch (start us, length us, event | category | flops | bytes accessed | tf_op | source)
XLA Modules:
  0.0 208.2 jit_solution(11612093982162679567)
XLA Ops:
  0.6 1.8 fusion.7
  3.8 6.5 %all-to-all-start.2 = ((bf16[128,16,256]{0,2,1:T(8,128)(2,1)}), bf16[128,16,256]{0,2,1:T(8,128)(2,1)S(1)}, u32[]{:S(2)}, u32[]{:S(2)}) async-start(bf16[128,16,256]{0,2,1:T(8,128)(2,1)} %bitcast.11), calls=%async_computation.2 | async-start | bytes 2097152 | tf_op jit(solution)/shard_map/all_to_all | solution.py:124
  10.3 8.2 %fusion.26 = bf16[16,128,256,1]{2,0,1,3:T(8,128)(2,1)} fusion(s32[128,256]{1,0:T(8,128)S(1)} %iota_subtract_fusion, bf16[256,128]{1,0:T(8,128)(2,1)S(1)} %copy-done, s32[]{:T(128)S(6)} %select_n.99), kind=kOutput, calls=%fused_computation.34 | convolution fusion | flops 138936320 | bytes 1183748 | tf_op jit(solution)/shard_map/while/body/eval_jaxpr/gj,tsj->gts/dot_general | solution.py:30
  18.5 16.7 %all-to-all-done.2 = bf16[128,16,256]{0,2,1:T(8,128)(2,1)S(1)} async-done(((bf16[128,16,256]{0,2,1:T(8,128)(2,1)}), bf16[128,16,256]{0,2,1:T(8,128)(2,1)S(1)}, u32[]{:S(2)}, u32[]{:S(2)}) %all-to-all-start.2) | async-done | bytes 1048608 | tf_op jit(solution)/shard_map/all_to_all | solution.py:124
  35.5 2.1 reshape.107
  37.6 4.0 %slice.28 = bf16[16,1,128,256]{2,1,3,0:T(2,128)(2,1)S(1)} slice(bf16[16,2,128,256]{2,1,3,0:T(2,128)(2,1)} %reshape.107), slice={[0:16], [1:2], [0:128], [0:256]} | slice | bytes 2097152 | tf_op jit(solution)/shard_map/while/body/eval_jaxpr/slice | solution.py:71
  46.9 2.3 %copy.66 = bf16[128,4096]{0,1:T(8,128)(2,1)} copy(bf16[128,4096]{1,0:T(8,128)(2,1)} %param.6) | data formatting | bytes 2097152 | tf_op args[1]
  49.2 2.3 %copy.67 = bf16[128,4096]{0,1:T(8,128)(2,1)} copy(bf16[128,4096]{1,0:T(8,128)(2,1)} %param.7) | data formatting | bytes 2097152 | tf_op args[2]
  51.4 1.8 collective-permute-start.2
  55.7 2.9 %collective-permute-start.6 = (f32[128,256]{0,1:T(8,128)}, f32[128,256]{0,1:T(8,128)S(1)}, u32[]{:S(2)}, u32[]{:S(2)}) collective-permute-start(f32[128,256]{0,1:T(8,128)} %get-tuple-element.46), channel_id=1, source_target_pairs={{0,7},{1,6},{2,5},{3,4},{4,3},{5,2},{6,1},{7,0},{8,15},{9,14},{10,... | collective-permute-start | bytes 393224 | tf_op jit(solution)/shard_map/ppermute | solution.py:22
  63.4 3.7 %collective-permute-done.5 = f32[128,256]{0,1:T(8,128)S(1)} collective-permute-done((f32[128,256]{0,1:T(8,128)}, f32[128,256]{0,1:T(8,128)S(1)}, u32[]{:S(2)}, u32[]{:S(2)}) %collective-permute-start.5) | collective-permute-done | bytes 131104 | tf_op jit(solution)/shard_map/ppermute | solution.py:22
  67.1 5.0 %collective-permute-start.10 = (f32[128,256]{0,1:T(8,128)}, f32[128,256]{0,1:T(8,128)S(1)}, u32[]{:S(2)}, u32[]{:S(2)}) collective-permute-start(f32[128,256]{0,1:T(8,128)} %get-tuple-element.42), channel_id=1, source_target_pairs={{0,11},{1,10},{2,9},{3,8},{4,15},{5,14},{6,13},{7,12},{8,3},{9,2},... | collective-permute-start | bytes 393224 | tf_op jit(solution)/shard_map/ppermute | solution.py:22
  73.5 10.2 %collective-permute-done.8 = f32[128,256]{0,1:T(8,128)S(1)} collective-permute-done((f32[128,256]{0,1:T(8,128)}, f32[128,256]{0,1:T(8,128)S(1)}, u32[]{:S(2)}, u32[]{:S(2)}) %collective-permute-start.8) | collective-permute-done | bytes 131104 | tf_op jit(solution)/shard_map/ppermute | solution.py:22
  83.7 2.9 %collective-permute-done.9 = f32[128,256]{0,1:T(8,128)S(1)} collective-permute-done((f32[128,256]{0,1:T(8,128)}, f32[128,256]{0,1:T(8,128)S(1)}, u32[]{:S(2)}, u32[]{:S(2)}) %collective-permute-start.9) | collective-permute-done | bytes 131104 | tf_op jit(solution)/shard_map/ppermute | solution.py:22
  87.6 4.5 %collective-permute-done.10 = f32[128,256]{0,1:T(8,128)S(1)} collective-permute-done((f32[128,256]{0,1:T(8,128)}, f32[128,256]{0,1:T(8,128)S(1)}, u32[]{:S(2)}, u32[]{:S(2)}) %collective-permute-start.10) | collective-permute-done | bytes 131104 | tf_op jit(solution)/shard_map/ppermute | solution.py:22
  92.1 6.4 %collective-permute-done.11 = f32[128,256]{0,1:T(8,128)S(1)} collective-permute-done((f32[128,256]{0,1:T(8,128)}, f32[128,256]{0,1:T(8,128)S(1)}, u32[]{:S(2)}, u32[]{:S(2)}) %collective-permute-start.11) | collective-permute-done | bytes 131104 | tf_op jit(solution)/shard_map/ppermute | solution.py:22
  98.5 3.1 %collective-permute-done.12 = f32[128,256]{0,1:T(8,128)S(1)} collective-permute-done((f32[128,256]{0,1:T(8,128)}, f32[128,256]{0,1:T(8,128)S(1)}, u32[]{:S(2)}, u32[]{:S(2)}) %collective-permute-start.12) | collective-permute-done | bytes 131104 | tf_op jit(solution)/shard_map/ppermute | solution.py:22
  101.6 2.8 %collective-permute-done.13 = f32[128,256]{0,1:T(8,128)S(1)} collective-permute-done((f32[128,256]{0,1:T(8,128)S(1)}, f32[128,256]{0,1:T(8,128)S(1)}, u32[]{:S(2)}, u32[]{:S(2)}) %collective-permute-start.13) | collective-permute-done | bytes 131104 | tf_op jit(solution)/shard_map/ppermute | solution.py:22
  104.5 2.8 %collective-permute-done.14 = f32[128,256]{0,1:T(8,128)S(1)} collective-permute-done((f32[128,256]{0,1:T(8,128)S(1)}, f32[128,256]{0,1:T(8,128)S(1)}, u32[]{:S(2)}, u32[]{:S(2)}) %collective-permute-start.14) | collective-permute-done | bytes 131104 | tf_op jit(solution)/shard_map/ppermute | solution.py:22
  107.3 2.1 fusion.8
  109.4 5.0 %all-to-all-start = ((bf16[128,16,256]{0,2,1:T(8,128)(2,1)}), bf16[128,16,256]{0,2,1:T(8,128)(2,1)S(1)}, u32[]{:S(2)}, u32[]{:S(2)}) async-start(bf16[128,16,256]{0,2,1:T(8,128)(2,1)} %bitcast.56), calls=%async_computation | async-start | bytes 2097152 | tf_op jit(solution)/shard_map/all_to_all | solution.py:123
  114.5 8.2 %fusion.25 = bf16[16,128,256,1]{2,0,1,3:T(8,128)(2,1)} fusion(s32[128,256]{1,0:T(8,128)S(1)} %iota_subtract_fusion.1, bf16[256,128]{1,0:T(8,128)(2,1)S(1)} %copy-done, s32[]{:T(128)S(6)} %select_n.99), kind=kOutput, calls=%fused_computation.33 | convolution fusion | flops 138936320 | bytes 1183748 | tf_op jit(solution)/shard_map/while/body/eval_jaxpr/gj,tsj->gts/dot_general | solution.py:30
  122.7 16.6 %all-to-all-done = bf16[128,16,256]{0,2,1:T(8,128)(2,1)S(1)} async-done(((bf16[128,16,256]{0,2,1:T(8,128)(2,1)}), bf16[128,16,256]{0,2,1:T(8,128)(2,1)S(1)}, u32[]{:S(2)}, u32[]{:S(2)}) %all-to-all-start) | async-done | bytes 1048608 | tf_op jit(solution)/shard_map/all_to_all | solution.py:123
  140.9 3.9 %copy.68 = bf16[16,256,256]{2,1,0:T(8,128)(2,1)} copy(bf16[16,256,256]{1,2,0:T(8,128)(2,1)} %fusion.12) | data formatting | bytes 4194304 | tf_op jit(solution)/shard_map/while/body/eval_jaxpr/concatenate | solution.py:66
  144.8 2.3 %slice.26 = bf16[16,1,128,256]{3,2,1,0:T(8,128)(2,1)} slice(bf16[16,2,128,256]{3,2,1,0:T(8,128)(2,1)} %bitcast.53), slice={[0:16], [0:1], [0:128], [0:256]} | slice | bytes 2097152 | tf_op jit(solution)/shard_map/while/body/eval_jaxpr/slice | solution.py:70
  148.8 2.3 %fusion.17 = f32[16,128,16,16]{1,3,0,2:T(8,128)S(1)} fusion(bf16[16,128,256,1]{2,0,1,3:T(8,128)(2,1)} %fusion.25, bf16[16,128,16,16]{1,3,2,0:T(8,128)(2,1)S(1)} %bitcast.46, bf16[16,128,16,16]{1,3,2,0:T(8,128)(2,1)S(1)} %bitcast.54), kind=kOutput, calls=%fused_computation.29 | convolution fusion | flops 272629760 | bytes 5242880 | tf_op jit(solution)/shard_map/while/body/eval_jaxpr/gts,bsgc->btgc/dot_general | solution.py:48
  152.7 4.8 %all-to-all-start.1 = ((f32[16,128,256]{1,2,0:T(8,128)}), f32[16,128,256]{1,2,0:T(8,128)}, u32[]{:S(2)}, u32[]{:S(2)}) async-start(f32[16,128,256]{1,2,0:T(8,128)} %bitcast.49), calls=%async_computation.1 | async-start | bytes 4194304 | tf_op jit(solution)/shard_map/all_to_all | solution.py:143
  157.5 2.4 %copy.82 = bf16[128,4096]{1,0:T(8,128)(2,1)} copy(bf16[128,4096]{0,1:T(8,128)(2,1)} %get-tuple-element.36) | data formatting | bytes 2097152
  164.3 3.6 %reshape.109 = f32[16,128,257]{2,1,0:T(8,128)} reshape(f32[16,32896]{1,0:T(8,128)S(1)} %pad.7) | data formatting | bytes 4210688 | tf_op jit(solution)/shard_map/while/body/eval_jaxpr/reshape | solution.py:56
  167.9 1.9 slice_reduce_fusion
  170.5 34.5 %all-to-all-done.1 = f32[16,128,256]{1,2,0:T(8,128)} async-done(((f32[16,128,256]{1,2,0:T(8,128)}), f32[16,128,256]{1,2,0:T(8,128)}, u32[]{:S(2)}, u32[]{:S(2)}) %all-to-all-start.1) | async-done | bytes 2097184 | tf_op jit(solution)/shard_map/all_to_all | solution.py:143
  205.0 2.0 copy.74
  (71 shorter events, 27.7 us)
Async XLA Ops:
  0.6 9.7 %copy-start = (bf16[256,128]{1,0:T(8,128)(2,1)S(1)}, bf16[256,128]{1,0:T(8,128)(2,1)}, u32[]{:S(2)}) copy-start(bf16[256,128]{1,0:T(8,128)(2,1)} %param.9) | copy-start | bytes 196612
  3.8 31.4 %all-to-all-start.2 = ((bf16[128,16,256]{0,2,1:T(8,128)(2,1)}), bf16[128,16,256]{0,2,1:T(8,128)(2,1)S(1)}, u32[]{:S(2)}, u32[]{:S(2)}) async-start(bf16[128,16,256]{0,2,1:T(8,128)(2,1)} %bitcast.11), calls=%async_computation.2 | async-start | bytes 2097152 | tf_op jit(solution)/shard_map/all_to_all | solution.py:124
  41.6 1.2 copy-start.6
  46.5 8.1 %collective-permute-start = (f32[128,256]{0,1:T(8,128)}, f32[128,256]{0,1:T(8,128)}, u32[]{:S(2)}, u32[]{:S(2)}) collective-permute-start(f32[128,256]{0,1:T(8,128)} %get-tuple-element.52), channel_id=1, source_target_pairs={{0,1},{1,0},{2,3},{3,2},{4,5},{5,4},{6,7},{7,6},{8,9},{9,8},{10,11... | collective-permute-start | bytes 393224 | tf_op jit(solution)/shard_map/ppermute | solution.py:22
  46.7 9.0 %collective-permute-start.1 = (f32[128,256]{0,1:T(8,128)}, f32[128,256]{0,1:T(8,128)}, u32[]{:S(2)}, u32[]{:S(2)}) collective-permute-start(f32[128,256]{0,1:T(8,128)} %get-tuple-element.51), channel_id=1, source_target_pairs={{0,2},{1,3},{2,0},{3,1},{4,6},{5,7},{6,4},{7,5},{8,10},{9,11},{10,... | collective-permute-start | bytes 393224 | tf_op jit(solution)/shard_map/ppermute | solution.py:22
  51.4 55.8 %copy-start.1 = (bf16[128,4096]{0,1:T(8,128)(2,1)S(1)}, bf16[128,4096]{0,1:T(8,128)(2,1)}, u32[]{:S(2)}) copy-start(bf16[128,4096]{0,1:T(8,128)(2,1)} %copy.66) | copy-start | bytes 3145732
  51.4 55.8 %copy-start.2 = (bf16[128,4096]{0,1:T(8,128)(2,1)S(1)}, bf16[128,4096]{0,1:T(8,128)(2,1)}, u32[]{:S(2)}) copy-start(bf16[128,4096]{0,1:T(8,128)(2,1)} %copy.67) | copy-start | bytes 3145732
  51.4 8.1 %collective-permute-start.2 = (f32[128,256]{0,1:T(8,128)}, f32[128,256]{0,1:T(8,128)S(1)}, u32[]{:S(2)}, u32[]{:S(2)}) collective-permute-start(f32[128,256]{0,1:T(8,128)} %get-tuple-element.50), channel_id=1, source_target_pairs={{0,3},{1,2},{2,1},{3,0},{4,7},{5,6},{6,5},{7,4},{8,11},{9,10},{10,... | collective-permute-start | bytes 393224 | tf_op jit(solution)/shard_map/ppermute | solution.py:22
  53.2 7.6 %collective-permute-start.3 = (f32[128,256]{0,1:T(8,128)}, f32[128,256]{0,1:T(8,128)S(1)}, u32[]{:S(2)}, u32[]{:S(2)}) collective-permute-start(f32[128,256]{0,1:T(8,128)} %get-tuple-element.49), channel_id=1, source_target_pairs={{0,4},{1,5},{2,6},{3,7},{4,0},{5,1},{6,2},{7,3},{8,12},{9,13},{10,... | collective-permute-start | bytes 393224 | tf_op jit(solution)/shard_map/ppermute | solution.py:22
  53.2 8.9 %collective-permute-start.4 = (f32[128,256]{0,1:T(8,128)}, f32[128,256]{0,1:T(8,128)S(1)}, u32[]{:S(2)}, u32[]{:S(2)}) collective-permute-start(f32[128,256]{0,1:T(8,128)} %get-tuple-element.48), channel_id=1, source_target_pairs={{0,5},{1,4},{2,7},{3,6},{4,1},{5,0},{6,3},{7,2},{8,13},{9,12},{10,... | collective-permute-start | bytes 393224 | tf_op jit(solution)/shard_map/ppermute | solution.py:22
  54.7 12.4 %collective-permute-start.5 = (f32[128,256]{0,1:T(8,128)}, f32[128,256]{0,1:T(8,128)S(1)}, u32[]{:S(2)}, u32[]{:S(2)}) collective-permute-start(f32[128,256]{0,1:T(8,128)} %get-tuple-element.47), channel_id=1, source_target_pairs={{0,6},{1,7},{2,4},{3,5},{4,2},{5,3},{6,0},{7,1},{8,14},{9,15},{10,... | collective-permute-start | bytes 393224 | tf_op jit(solution)/shard_map/ppermute | solution.py:22
  55.7 16.5 %collective-permute-start.6 = (f32[128,256]{0,1:T(8,128)}, f32[128,256]{0,1:T(8,128)S(1)}, u32[]{:S(2)}, u32[]{:S(2)}) collective-permute-start(f32[128,256]{0,1:T(8,128)} %get-tuple-element.46), channel_id=1, source_target_pairs={{0,7},{1,6},{2,5},{3,4},{4,3},{5,2},{6,1},{7,0},{8,15},{9,14},{10,... | collective-permute-start | bytes 393224 | tf_op jit(solution)/shard_map/ppermute | solution.py:22
  59.5 12.7 %collective-permute-start.7 = (f32[128,256]{0,1:T(8,128)}, f32[128,256]{0,1:T(8,128)S(1)}, u32[]{:S(2)}, u32[]{:S(2)}) collective-permute-start(f32[128,256]{0,1:T(8,128)} %get-tuple-element.45), channel_id=1, source_target_pairs={{0,8},{1,9},{2,10},{3,11},{4,12},{5,13},{6,14},{7,15},{8,0},{9,1},... | collective-permute-start | bytes 393224 | tf_op jit(solution)/shard_map/ppermute | solution.py:22
  60.8 22.9 %collective-permute-start.8 = (f32[128,256]{0,1:T(8,128)}, f32[128,256]{0,1:T(8,128)S(1)}, u32[]{:S(2)}, u32[]{:S(2)}) collective-permute-start(f32[128,256]{0,1:T(8,128)} %get-tuple-element.44), channel_id=1, source_target_pairs={{0,9},{1,8},{2,11},{3,10},{4,13},{5,12},{6,15},{7,14},{8,1},{9,0},... | collective-permute-start | bytes 393224 | tf_op jit(solution)/shard_map/ppermute | solution.py:22
  62.1 24.5 %collective-permute-start.9 = (f32[128,256]{0,1:T(8,128)}, f32[128,256]{0,1:T(8,128)S(1)}, u32[]{:S(2)}, u32[]{:S(2)}) collective-permute-start(f32[128,256]{0,1:T(8,128)} %get-tuple-element.43), channel_id=1, source_target_pairs={{0,10},{1,11},{2,8},{3,9},{4,14},{5,15},{6,12},{7,13},{8,2},{9,3},... | collective-permute-start | bytes 393224 | tf_op jit(solution)/shard_map/ppermute | solution.py:22
  67.1 25.0 %collective-permute-start.10 = (f32[128,256]{0,1:T(8,128)}, f32[128,256]{0,1:T(8,128)S(1)}, u32[]{:S(2)}, u32[]{:S(2)}) collective-permute-start(f32[128,256]{0,1:T(8,128)} %get-tuple-element.42), channel_id=1, source_target_pairs={{0,11},{1,10},{2,9},{3,8},{4,15},{5,14},{6,13},{7,12},{8,3},{9,2},... | collective-permute-start | bytes 393224 | tf_op jit(solution)/shard_map/ppermute | solution.py:22
  72.2 26.3 %collective-permute-start.11 = (f32[128,256]{0,1:T(8,128)}, f32[128,256]{0,1:T(8,128)S(1)}, u32[]{:S(2)}, u32[]{:S(2)}) collective-permute-start(f32[128,256]{0,1:T(8,128)} %get-tuple-element.41), channel_id=1, source_target_pairs={{0,12},{1,13},{2,14},{3,15},{4,8},{5,9},{6,10},{7,11},{8,4},{9,5},... | collective-permute-start | bytes 393224 | tf_op jit(solution)/shard_map/ppermute | solution.py:22
  72.3 29.3 %collective-permute-start.12 = (f32[128,256]{0,1:T(8,128)}, f32[128,256]{0,1:T(8,128)S(1)}, u32[]{:S(2)}, u32[]{:S(2)}) collective-permute-start(f32[128,256]{0,1:T(8,128)} %get-tuple-element.40), channel_id=1, source_target_pairs={{0,13},{1,12},{2,15},{3,14},{4,9},{5,8},{6,11},{7,10},{8,5},{9,4},... | collective-permute-start | bytes 393224 | tf_op jit(solution)/shard_map/ppermute | solution.py:22
  83.7 20.8 %collective-permute-start.13 = (f32[128,256]{0,1:T(8,128)S(1)}, f32[128,256]{0,1:T(8,128)S(1)}, u32[]{:S(2)}, u32[]{:S(2)}) collective-permute-start(f32[128,256]{0,1:T(8,128)S(1)} %get-tuple-element.39), channel_id=1, source_target_pairs={{0,14},{1,15},{2,12},{3,13},{4,10},{5,11},{6,8},{7,9},{8,6},{9,7},... | collective-permute-start | bytes 393224 | tf_op jit(solution)/shard_map/ppermute | solution.py:22
  86.6 20.6 %collective-permute-start.14 = (f32[128,256]{0,1:T(8,128)S(1)}, f32[128,256]{0,1:T(8,128)S(1)}, u32[]{:S(2)}, u32[]{:S(2)}) collective-permute-start(f32[128,256]{0,1:T(8,128)S(1)} %get-tuple-element.38), channel_id=1, source_target_pairs={{0,15},{1,14},{2,13},{3,12},{4,11},{5,10},{6,9},{7,8},{8,7},{9,6},... | collective-permute-start | bytes 393224 | tf_op jit(solution)/shard_map/ppermute | solution.py:22
  109.4 29.9 %all-to-all-start = ((bf16[128,16,256]{0,2,1:T(8,128)(2,1)}), bf16[128,16,256]{0,2,1:T(8,128)(2,1)S(1)}, u32[]{:S(2)}, u32[]{:S(2)}) async-start(bf16[128,16,256]{0,2,1:T(8,128)(2,1)} %bitcast.56), calls=%async_computation | async-start | bytes 2097152 | tf_op jit(solution)/shard_map/all_to_all | solution.py:123
  148.8 2.3 %copy-start.4 = (bf16[16,1,128,256]{2,3,0,1:T(8,128)(2,1)}, bf16[16,1,128,256]{2,3,0,1:T(8,128)(2,1)S(1)}, u32[]{:S(2)}) copy-start(bf16[16,1,128,256]{2,3,0,1:T(8,128)(2,1)S(1)} %copy.69) | copy-start | bytes 3145732
  152.7 52.4 %all-to-all-start.1 = ((f32[16,128,256]{1,2,0:T(8,128)}), f32[16,128,256]{1,2,0:T(8,128)}, u32[]{:S(2)}, u32[]{:S(2)}) async-start(f32[16,128,256]{1,2,0:T(8,128)} %bitcast.49), calls=%async_computation.1 | async-start | bytes 4194304 | tf_op jit(solution)/shard_map/all_to_all | solution.py:143
  157.5 2.4 %copy-start.3 = (bf16[128,4096]{0,1:T(8,128)(2,1)S(1)}, bf16[128,4096]{0,1:T(8,128)(2,1)}, u32[]{:S(2)}) copy-start(bf16[128,4096]{0,1:T(8,128)(2,1)} %get-tuple-element.26) | copy-start | bytes 3145732
  205.0 2.0 copy-start.5
